TPU v7x, 128 devices: a whole 4x4x4 slice. The times are simulated.
128 devices in a mesh: band: 4 (over z_lo, core), slab: 32 (over x, y, z_hi).
Axes of the slice: x: 4, y: 4, z: 4 (z_hi: 2, z_lo: 2; z = z_hi * 2 + z_lo), core: 2. Of those that a mesh axis runs over, the one named last changes fastest.
Arguments:
- current_image: float32 [8, 4, 2, 128, 384], P('band', None, None, 'slab'), may hold values from -6 to 6
- langevin_noise: float32 [8, 4, 2, 128, 384], P('band', None, None, 'slab'), may hold values from -6 to 6
- step_size: float32 [1], replicated, may hold values from 0.2 to 0.5
- coil_maps: bfloat16 [8, 4, 32, 2, 128, 384], P(None, None, 'band', None, 'slab'), may hold values from -1 to 1
- measured_kspace: float32 [4, 32, 2, 128, 384], P(None, 'band', None, 'slab'), may hold values from -6 to 6
- sample_mask: int32 [4, 384], replicated, may hold values 0 or 1
- caipi_steps: int32 [8], replicated, may hold values from 0 to 7
- band_order: int32 [8], replicated, may hold values from 0 to 7, each once
- weight_in: bfloat16 [64, 2, 3, 3, 3], replicated, may hold values from -0.875 to 0.875
- weight_mid: bfloat16 [64, 64, 3, 3, 3], replicated, may hold values from -0.15625 to 0.15625
- weight_out: bfloat16 [2, 64, 3, 3, 3], replicated, may hold values from -0.359375 to 0.359375
Outputs:
- next_image: float32 [8, 4, 2, 128, 384], P('band', None, None, 'slab')
Inputs may be any that keep to these rules, and one draw needn't show every extreme that they name: `sample_mask`: 1 where a phase-encode line of a slice group was sampled, else 0. `caipi_steps`: shift of a band in units of 48 columns. `band_order`: a permutation of 0 to 7.
All inputs are finite; a program needn't handle non-finite values.
Results may differ from a plain program's by a relative error of at most 0.0039.
Values may be sent and summed in bfloat16 or wider, within the bound.
A program may use at most 128 MiB of HBM per device.

v0:
```python
import functools
import math

import jax
import jax.numpy as jnp
import numpy as np
from jax import lax
from jax.experimental import pallas as pl
from jax.experimental.pallas import tpu as pltpu
from jax.sharding import PartitionSpec as P

MESH = pl.DeviceIdType.MESH
F32 = jnp.float32
BF16 = jnp.bfloat16
NB, NS, Y, NC, CH, ROWS = 8, 4, 384, 8, 64, 4
Q = Y // 16
LEAD = (2, 3, 4)


def column_of():
    p = np.arange(Y)
    return (p % 16) * Q + p // 16


def constants():
    col = column_of()
    perm = np.zeros((3, Y, Y), np.float32)
    for dx in range(3):
        for p in range(Y):
            c = col[p] + dx - 1
            if 0 <= c < Y:
                perm[dx, p, c] = 1.0
    k = np.arange(Y)
    phase = (np.outer(k, k) % Y).astype(np.float64) * (2.0 * math.pi / Y)
    table = np.concatenate([np.cos(phase), np.sin(phase)], axis=1) / math.sqrt(Y)
    table = table.astype(np.float32)
    high = table.astype(BF16)
    low = (table - high.astype(np.float32)).astype(BF16)
    row_at = [0, 1, 2, 3, -2, -1, 4, 5]
    place_in = np.zeros((6, 144, 54), np.float32)
    for ro in range(6):
        for dz in range(3):
            for dx in range(3):
                for ch in range(2):
                    for i, row in enumerate(row_at):
                        dy = row - (ro - 1) + 1
                        if 0 <= dy <= 2:
                            t = ((dz * 3 + dy) * 3 + dx) * 2 + ch
                            place_in[ro, dz * 48 + dx * 16 + ch * 8 + i, t] = 0.5
    place_out = np.zeros((4, 144, 54), np.float32)
    for rin in range(4):
        for dz in range(3):
            for dx in range(3):
                for ch in range(2):
                    for ro in range(-1, 5):
                        dy = rin - ro + 1
                        if 0 <= dy <= 2:
                            t = ((dz * 3 + dy) * 3 + dx) * 2 + ch
                            if ro == -1:
                                m = 8 + ch
                            elif ro == 4:
                                m = 10 + ch
                            else:
                                m = ch * 4 + ro
                            place_out[rin, (dz * 3 + dx) * 16 + m, t] = 1.0
    return (
        perm.reshape(3 * Y, Y).astype(BF16),
        high,
        low,
        place_in.astype(BF16),
        place_out.astype(BF16),
    )


def dot_nn(a, b):
    return jnp.dot(a, b, preferred_element_type=F32)


def dot_nt(a, b):
    return lax.dot_general(a, b, (((1,), (1,)), ((), ())), preferred_element_type=F32)


def dot_tn(a, b):
    return lax.dot_general(a, b, (((0,), (0,)), ((), ())), preferred_element_type=F32)


def kernel(
    image, coil, measured, mask_in, steps_in, order_in, w_in, w_mid, w_out,
    perm_in, high_in, low_in, place1_in, place3_in,
    out,
    img, imgbuf, hsend, hrecv, dsend, drecv,
    rsend, rrecv, zsend, zrecv, esend, erecv, csend, crecv,
    coilv, rolled, meas, maskv, steps, order, win, wmid, wout,
    perm, high, low, place1, place3,
    w1, w2, w3, rimg, data, xp, f1, f2, gsum, score, cons,
    local, send_a, recv_a, send_h, recv_h, send_d, recv_d,
    send_r, recv_r, send_z, recv_z, send_e, recv_e, send_c, recv_c,
):
    b = lax.axis_index("band")
    s = lax.axis_index("slab")
    nb = lax.axis_size("band")
    ns = lax.axis_size("slab")

    def at(db, ds_):
        return {"band": lax.rem(b + db + nb, nb), "slab": lax.rem(s + ds_ + ns, ns)}

    partners = [at(k, 0) for k in range(1, nb)] + [at(0, -1), at(0, 1)]
    partners += [at(db, ds_) for db in (-1, 1) for ds_ in (-1, 1)]
    barrier = pltpu.get_barrier_semaphore()
    for who in partners:
        pl.semaphore_signal(barrier, inc=1, device_id=who, device_id_type=MESH)

    groups = {}

    def fetch(name, index, pairs):
        copies = [pltpu.make_async_copy(src, dst, local.at[index, i]) for i, (src, dst) in enumerate(pairs)]
        for c in copies:
            c.start()
        groups[name] = copies

    def arrived(name):
        for c in groups.pop(name):
            c.wait()

    fetch("image", 0, [(image.at[g, t], img.at[g, :, pl.ds(4 * t, 4), :]) for g in range(2) for t in range(4)])
    fetch("scalars", 1, [(steps_in, steps), (order_in, order)])
    for g in range(NB):
        fetch(
            f"coil{g}",
            2 + g,
            [
                (coil.at[g, t, :, r], coilv.at[g, :, r, pl.ds(4 * t, 4), :])
                for t in range(4)
                for r in range(2)
            ],
        )
    fetch("weights", 10, [(w_in, win), (w_mid, wmid), (w_out, wout), (place1_in, place1), (place3_in, place3)])
    fetch("perm", 11, [(perm_in, perm)])
    fetch("tables", 12, [(high_in, high), (low_in, low), (mask_in, maskv)])
    fetch(
        "meas",
        13,
        [(measured.at[t, :, r], meas.at[r, :, pl.ds(4 * t, 4), :]) for t in range(4) for r in range(2)],
    )

    arrived("image")
    own = pl.multiple_of(2 * b, 2)
    for g in range(2):
        for r in range(2):
            imgbuf[own + g, r] = img[g, r].astype(BF16)
    for side in range(2):
        rows = [
            [img[g, r, 4 * t + 2 * side : 4 * t + 2 * side + 2, :] for g in range(2) for t in range(4)]
            for r in range(2)
        ]
        for r in range(2):
            hsend[side, r] = jnp.concatenate(rows[r], axis=0).astype(BF16)
        for zside in range(2):
            z0 = 0 if zside == 0 else 6
            dsend[side, zside] = jnp.concatenate(
                [rows[0][z0], rows[0][z0 + 1], rows[1][z0], rows[1][z0 + 1]], axis=0
            ).astype(BF16)

    def remote(src, dst, ssem, rsem, who):
        return pltpu.make_async_remote_copy(
            src_ref=src, dst_ref=dst, send_sem=ssem, recv_sem=rsem, device_id=who, device_id_type=MESH
        )

    pl.semaphore_wait(barrier, len(partners))
    halo_copies = []
    for side in range(2):
        ds_ = -1 if side == 0 else 1
        halo_copies.append(
            remote(hsend.at[side], hrecv.at[1 - side], send_h.at[side], recv_h.at[1 - side], at(0, ds_))
        )
        for zside in range(2):
            db = -1 if zside == 0 else 1
            i, j = side * 2 + zside, (1 - side) * 2 + (1 - zside)
            halo_copies.append(
                remote(dsend.at[side, zside], drecv.at[1 - side, 1 - zside], send_d.at[i], recv_d.at[j], at(db, ds_))
            )
    image_copies = [
        remote(
            imgbuf.at[pl.ds(own, 2)], imgbuf.at[pl.ds(own, 2)], send_a.at[k - 1], recv_a.at[k - 1], at(k, 0)
        )
        for k in range(1, nb)
    ]
    for c in halo_copies + image_copies:
        c.start()

    arrived("scalars")
    shifts = [steps[order[g]] * (Y // 8) for g in range(NB)]
    for g in range(NB):
        arrived(f"coil{g}")
        for c in range(NC):
            for r in range(2):
                rolled[g, c, r] = pltpu.roll(coilv[g, c, r], shifts[g], 1)

    arrived("weights")
    lane = lax.broadcasted_iota(jnp.int32, (1, 6 * CH), 1)
    inside = ((lane >= CH) | (s > 0)) & ((lane < 5 * CH) | (s < ns - 1))
    w1v = jnp.concatenate([dot_nn(place1[r], win[...]) for r in range(6)], axis=1)
    w1[...] = jnp.where(inside, w1v, 0.0).astype(BF16)
    w3[...] = jnp.concatenate([dot_nn(place3[r], wout[...]) for r in range(4)], axis=1).astype(BF16)
    none = jnp.zeros((CH, CH), F32)
    for dx in range(3):
        for dz in range(3):
            taps = [wmid[(dz * 3 + dy) * 3 + dx].astype(F32) * 0.5 for dy in range(3)]
            for ro in range(2):
                block = taps + [none] if ro == 0 else [none] + taps
                block = jnp.concatenate(block, axis=1).astype(BF16)
                for sl in range(2):
                    k = dx * 4 + dz + sl
                    w2[pl.ds(sl * 128 + ro * CH, CH), pl.ds(k * 256, 256)] = block
        w2[pl.ds(128, 128), pl.ds((dx * 4) * 256, 256)] = jnp.zeros((128, 256), BF16)
        w2[pl.ds(0, 128), pl.ds((dx * 4 + 3) * 256, 256)] = jnp.zeros((128, 256), BF16)

    for c in image_copies:
        c.wait_recv()
    for g in range(NB):
        for r in range(2):
            rimg[g, r] = pltpu.roll(imgbuf[g, r].astype(F32), shifts[g], 1)

    def collapse(c, carry):
        real = jnp.zeros((16, Y), F32)
        imag = jnp.zeros((16, Y), F32)
        for g in range(NB):
            a_re = rolled[g, c, 0].astype(F32)
            a_im = rolled[g, c, 1].astype(F32)
            b_re = rimg[g, 0]
            b_im = rimg[g, 1]
            real += a_re * b_re - a_im * b_im
            imag += a_re * b_im + a_im * b_re
        data[0, c] = real
        data[1, c] = imag
        return carry

    lax.fori_loop(0, NC, collapse, 0)

    for c in halo_copies:
        c.wait_recv()
    arrived("perm")
    low_ok, high_ok = s > 0, s < ns - 1
    tiles = []
    for i in range(12):
        z = i - 2
        pieces = []
        if z < 0:
            slot = lax.max(2 * b - 1, 0)
            t = 4 + z
            ok = b > 0
            halo = [drecv[side, 0] for side in range(2)]
            offset, stride = (z + 2) * 2, 4
        elif z > 7:
            slot = lax.min(2 * b + 2, NB - 1)
            t = z - 8
            ok = b < nb - 1
            halo = [drecv[side, 1] for side in range(2)]
            offset, stride = (z - 8) * 2, 4
        else:
            slot = own + z // 4
            t = z % 4
            ok = None
            halo = None
        for r in range(2):
            mine = imgbuf[slot, r].astype(F32)[4 * t : 4 * t + 4, :]
            if halo is None:
                below = hrecv[0, r].astype(F32)[2 * z : 2 * z + 2, :]
                above = hrecv[1, r].astype(F32)[2 * z : 2 * z + 2, :]
            else:
                o = r * stride + offset
                below = halo[0].astype(F32)[o : o + 2, :]
                above = halo[1].astype(F32)[o : o + 2, :]
            below = jnp.where(low_ok, below, 0.0)
            above = jnp.where(high_ok, above, 0.0)
            pieces += [mine, below, above]
        tile = jnp.concatenate(pieces, axis=0)
        if ok is not None:
            tile = jnp.where(ok, tile, 0.0)
        tiles.append(tile.astype(BF16))
    field = jnp.concatenate(tiles, axis=0)
    for dx in range(3):
        moved = dot_nt(field, perm[pl.ds(dx * Y, Y), :]).astype(BF16)
        for i in range(12):
            xp[pl.ds(i * 48 + dx * 16, 16), :] = moved[16 * i : 16 * i + 16, :]

    sub = lax.broadcasted_iota(jnp.int32, (16, 6 * CH), 0)

    def first(z, carry):
        x = xp[pl.ds(pl.multiple_of(z * 48, 48), 144), :]
        inside_z = ((z > 0) | (b > 0)) & ((z < 9) | (b < nb - 1))
        x = jnp.where(inside_z, x, jnp.zeros_like(x))
        h = dot_tn(x, w1[...])
        f = h + h * jnp.tanh(h)
        f1[z, pl.ds(16, Y), :] = f.astype(BF16)
        left = jnp.where(sub == 0, 0.0, pltpu.roll(f[Y - 16 :, :], 1, 0))
        right = jnp.where(sub == 15, 0.0, pltpu.roll(f[:16, :], 15, 0))
        f1[z, pl.ds(0, 16), :] = left.astype(BF16)
        f1[z, pl.ds(Y + 16, 16), :] = right.astype(BF16)
        return carry

    lax.fori_loop(0, 10, first, 0)

    def middle(zp, carry):
        for rp in range(2):
            lhs = jnp.concatenate(
                [
                    f1[2 * zp + j, pl.ds(16 * dx, Y), pl.ds(rp * 128, 256)]
                    for dx in range(3)
                    for j in range(4)
                ],
                axis=1,
            )
            h = dot_nt(lhs, w2[...])
            f = (h + h * jnp.tanh(h)).astype(BF16)
            f2[2 * zp, :, pl.ds(rp * 128, 128)] = f[:, :128]
            f2[2 * zp + 1, :, pl.ds(rp * 128, 128)] = f[:, 128:]
        return carry

    lax.fori_loop(0, 4, middle, 0)

    gsum[...] = jnp.zeros_like(gsum)

    def last(z, carry):
        part = dot_nt(w3[...], f2[z])
        for dz in range(3):
            for dx in range(3):
                o = (dz * 3 + dx) * 16
                gsum[2 - dx, z + 2 - dz] += part[o : o + 16, :]
        return carry

    lax.fori_loop(0, 8, last, 0)
    total = gsum[...].reshape(3, 160, Y)
    top = total.astype(BF16)
    rest = (total - top.astype(F32)).astype(BF16)
    stacked = jnp.concatenate([jnp.concatenate([top[i], rest[i]], axis=0) for i in range(3)], axis=1)
    both = dot_nn(stacked, perm[...])
    score[...] = (both[:160] + both[160:]).reshape(10, 16, Y)

    for side in range(2):
        o = 8 + 2 * side
        rsend[side] = jnp.concatenate([score[z + 1, o : o + 2, :] for z in range(8)], axis=0).astype(BF16)
        zi = 0 if side == 0 else 9
        zsend[side] = score[zi, 0:8, :].astype(BF16)
        for rside in range(2):
            o = 8 + 2 * rside
            pad = jnp.zeros((6, Y), F32)
            esend[rside, side] = jnp.concatenate([score[zi, o : o + 2, :], pad], axis=0).astype(BF16)
    score_copies = []
    for side in range(2):
        d = -1 if side == 0 else 1
        score_copies.append(
            remote(rsend.at[side], rrecv.at[1 - side], send_r.at[side], recv_r.at[1 - side], at(0, d))
        )
        for zside in range(2):
            db = -1 if zside == 0 else 1
            i, j = side * 2 + zside, (1 - side) * 2 + (1 - zside)
            score_copies.append(
                remote(esend.at[side, zside], erecv.at[1 - side, 1 - zside], send_e.at[i], recv_e.at[j], at(db, d))
            )
    for side in range(2):
        d = -1 if side == 0 else 1
        score_copies.append(
            remote(zsend.at[side], zrecv.at[1 - side], send_z.at[side], recv_z.at[1 - side], at(d, 0))
        )
    for c in score_copies:
        c.start()

    arrived("tables")
    arrived("meas")

    def transform(field):
        flat = field.reshape(2 * NC * 16, Y)
        top = flat.astype(BF16)
        rest = (flat - top.astype(F32)).astype(BF16)
        lhs = jnp.concatenate([top, rest, top], axis=1)
        rhs = jnp.concatenate([high[...], high[...], low[...]], axis=0)
        both = dot_nn(lhs, rhs)
        half = NC * 16
        return both[:half, :Y], both[:half, Y:], both[half:, :Y], both[half:, Y:]

    re_c, re_s, im_c, im_s = transform(data[...])
    keep = maskv[...].astype(F32)
    keep = jnp.concatenate([jnp.broadcast_to(keep[t : t + 1], (4, Y)) for t in range(4)], axis=0)[None]
    data[0] = keep * ((re_c + im_s).reshape(NC, 16, Y) - meas[0])
    data[1] = keep * ((im_c - re_s).reshape(NC, 16, Y) - meas[1])
    re_c, re_s, im_c, im_s = transform(data[...])
    data[0] = (re_c - im_s).reshape(NC, 16, Y)
    data[1] = (im_c + re_s).reshape(NC, 16, Y)

    for g in range(NB):
        real = jnp.zeros((16, Y), F32)
        imag = jnp.zeros((16, Y), F32)
        for c in range(NC):
            a_re = rolled[g, c, 0].astype(F32)
            a_im = rolled[g, c, 1].astype(F32)
            real += a_re * data[0, c] + a_im * data[1, c]
            imag += a_re * data[1, c] - a_im * data[0, c]
        back = lax.rem(Y - shifts[g], Y)
        cons[g, 0] = pltpu.roll(real, back, 1)
        cons[g, 1] = pltpu.roll(imag, back, 1)
        csend[g, 0] = cons[g, 0].astype(BF16)
        csend[g, 1] = cons[g, 1].astype(BF16)
    cons_copies = []
    for k in range(1, nb):
        peer = lax.rem(b + k, nb)
        cons_copies.append(
            remote(
                csend.at[pl.ds(pl.multiple_of(2 * peer, 2), 2)],
                crecv.at[k - 1],
                send_c.at[k - 1],
                recv_c.at[k - 1],
                at(k, 0),
            )
        )
    for c in cons_copies:
        c.start()
    for c in halo_copies + image_copies:
        c.wait_send()

    for c in score_copies:
        c.wait_recv()
    for c in cons_copies:
        c.wait_recv()
    gap = jnp.zeros((2, Y), F32)
    for g in range(2):
        consistency = []
        for r in range(2):
            v = cons[own + g, r]
            for k in range(1, nb):
                v = v + crecv[k - 1, g, r].astype(F32)
            consistency.append(v)
        for t in range(4):
            z = g * 4 + t
            v = score[z + 1, 0:8, :]
            below = jnp.where(low_ok, rrecv[0].astype(F32)[2 * z : 2 * z + 2, :], 0.0)
            above = jnp.where(high_ok, rrecv[1].astype(F32)[2 * z : 2 * z + 2, :], 0.0)
            if z in (0, 7):
                zside = 0 if z == 0 else 1
                ok = b > 0 if z == 0 else b < nb - 1
                v = v + jnp.where(ok, zrecv[zside].astype(F32), 0.0)
                below = below + jnp.where(ok & low_ok, erecv[0, zside].astype(F32)[0:2, :], 0.0)
                above = above + jnp.where(ok & high_ok, erecv[1, zside].astype(F32)[0:2, :], 0.0)
            v = v + jnp.concatenate(
                [below[0:1], gap, above[0:1], below[1:2], gap, above[1:2]], axis=0
            )
            for r in range(2):
                out[g, t, r] = v[4 * r : 4 * r + 4, :] - consistency[r][4 * t : 4 * t + 4, :]
    for c in score_copies + cons_copies:
        c.wait_send()


def per_device(
    current_image,
    langevin_noise,
    step_size,
    coil_maps,
    measured_kspace,
    sample_mask,
    caipi_steps,
    band_order,
    weight_in,
    weight_mid,
    weight_out,
):
    w_in = jnp.transpose(weight_in, (2, 3, 4, 1, 0)).reshape(54, CH)
    w_mid = jnp.transpose(weight_mid, (2, 3, 4, 0, 1)).reshape(27, CH, CH)
    w_out = jnp.transpose(weight_out, (2, 3, 4, 0, 1)).reshape(54, CH)
    consts = [jnp.asarray(c) for c in constants()]
    dma = pltpu.SemaphoreType.DMA
    vmem = pltpu.VMEM
    tile = (16, Y)
    difference = pl.pallas_call(
        kernel,
        out_shape=jax.ShapeDtypeStruct(current_image.shape, F32),
        in_specs=[pl.BlockSpec(memory_space=pl.ANY)] * 14,
        out_specs=pl.BlockSpec(memory_space=pltpu.VMEM),
        scratch_shapes=[
            vmem((2, 2) + tile, F32),
            vmem((NB, 2) + tile, BF16),
            vmem((2, 2) + tile, BF16),
            vmem((2, 2) + tile, BF16),
            vmem((2, 2, 8, Y), BF16),
            vmem((2, 2, 8, Y), BF16),
            vmem((2,) + tile, BF16),
            vmem((2,) + tile, BF16),
            vmem((2, 8, Y), BF16),
            vmem((2, 8, Y), BF16),
            vmem((2, 2, 8, Y), BF16),
            vmem((2, 2, 8, Y), BF16),
            vmem((NB, 2) + tile, BF16),
            vmem((3, 2, 2) + tile, BF16),
            vmem((NB, NC, 2) + tile, BF16),
            vmem((NB, NC, 2) + tile, BF16),
            vmem((2, NC) + tile, F32),
            vmem((NS, Y), jnp.int32),
            pltpu.SMEM((NB,), jnp.int32),
            pltpu.SMEM((NB,), jnp.int32),
            vmem((54, CH), BF16),
            vmem((27, CH, CH), BF16),
            vmem((54, CH), BF16),
            vmem((3 * Y, Y), BF16),
            vmem((Y, 2 * Y), BF16),
            vmem((Y, 2 * Y), BF16),
            vmem((6, 144, 54), BF16),
            vmem((4, 144, 54), BF16),
            vmem((144, 6 * CH), BF16),
            vmem((256, 12 * 256), BF16),
            vmem((144, 4 * CH), BF16),
            vmem((NB, 2) + tile, F32),
            vmem((2, NC) + tile, F32),
            vmem((12 * 48, Y), BF16),
            vmem((10, Y + 32, 6 * CH), BF16),
            vmem((8, Y, 4 * CH), BF16),
            vmem((3, 10) + tile, F32),
            vmem((10,) + tile, F32),
            vmem((NB, 2) + tile, F32),
            dma((14, 8)),
            dma((3,)),
            dma((3,)),
            dma((2,)),
            dma((2,)),
            dma((4,)),
            dma((4,)),
            dma((2,)),
            dma((2,)),
            dma((2,)),
            dma((2,)),
            dma((4,)),
            dma((4,)),
            dma((3,)),
            dma((3,)),
        ],
        compiler_params=pltpu.CompilerParams(collective_id=0, has_side_effects=True),
        name="langevin",
    )(
        current_image, coil_maps, measured_kspace, sample_mask, caipi_steps, band_order,
        w_in, w_mid, w_out, *consts,
    )
    step_value = step_size[0]
    return current_image + step_value * difference + jnp.sqrt(2.0 * step_value) * langevin_noise


def solution(mesh):
    in_specs = (
        P("band", None, None, "slab", None),
        P("band", None, None, "slab", None),
        P(),
        P(None, None, "band", None, "slab", None),
        P(None, "band", None, "slab", None),
        P(),
        P(),
        P(),
        P(),
        P(),
        P(),
    )
    out_specs = P("band", None, None, "slab", None)
    return jax.shard_map(
        per_device, mesh=mesh, in_specs=in_specs, out_specs=out_specs, check_vma=False
    )
```

profile of v0, /device:TPU:1, one launch (start us, length us, event | category | flops | bytes accessed | tf_op | source)
XLA Modules:
  0.0 39.8 jit_solution(486304363309116761)
XLA Ops:
  0.7 1.3 %reshape.9.w_in = bf16[54,64]{1,0:T(8,128)(2,1)} reshape(bf16[3,3,3,2,64]{4,3,2,1,0:T(2,128)(2,1)} %bitcast.16) | data formatting | bytes 13824 | tf_op jit(solution)/shard_map/reshape | solution.py:466
  2.0 1.3 %reshape.11.w_out = bf16[54,64]{1,0:T(8,128)(2,1)} reshape(bf16[3,3,3,2,64]{4,3,2,1,0:T(2,128)(2,1)} %bitcast.17) | data formatting | bytes 13824 | tf_op jit(solution)/shard_map/reshape | solution.py:468
  3.4 0.0 copy-start
  3.4 0.0 copy-start.1
  3.4 34.8 %langevin.1 = f32[2,4,2,4,384]{4,3,2,1,0:T(4,128)} custom-call(f32[2,4,2,4,384]{4,3,2,1,0:T(4,128)} %image.1, bf16[8,4,8,2,4,384]{5,4,3,2,1,0:T(4,128)(2,1)} %coil.1, f32[4,8,2,4,384]{4,3,2,1,0:T(4,128)} %measured.1, s32[4,384]{1,0:T(4,128)} %mask_in.1, s32[8]{0:T(128)} %steps_in.1, s32[8]{0:T(128)} %order_in.1, bf16[54,64]{1,0:T(8,128)(2,1)} %reshape.9.w_in, ...), custom_call_target="tpu_custom_call" | custom-call | tf_op jit(solution)/shard_map/langevin/pallas_call | solution.py:473
  38.2 0.0 copy-done
  38.2 0.0 copy-done.1
  38.2 1.6 %multiply_add_fusion = f32[2,4,1,8,384]{4,3,2,1,0:T(8,128)} fusion(f32[2,4,1,8,384]{4,3,2,1,0:T(8,128)S(1)} %bitcast.15, f32[2,4,1,8,384]{4,3,2,1,0:T(8,128)S(1)} %bitcast.13, f32[2,4,1,8,384]{4,3,2,1,0:T(8,128)} %bitcast.14, f32[]{:T(128)S(6)} %sqrt.3, f32[]{:T(128)} %bitcast.10), kind=kLoop, calls=%fused_computation | loop fusion | flops 98304 | bytes 393224 | tf_op jit(solution)/shard_map/add | solution.py:541
Async XLA Ops:
  3.4 34.8 %copy-start = (f32[2,4,2,4,384]{4,3,2,1,0:T(4,128)S(1)}, f32[2,4,2,4,384]{4,3,2,1,0:T(4,128)}, u32[]{:S(2)}) copy-start(f32[2,4,2,4,384]{4,3,2,1,0:T(4,128)} %image.1) | copy-start | bytes 294916
  3.4 34.9 %copy-start.1 = (f32[2,4,2,4,384]{4,3,2,1,0:T(4,128)S(1)}, f32[2,4,2,4,384]{4,3,2,1,0:T(4,128)}, u32[]{:S(2)}) copy-start(f32[2,4,2,4,384]{4,3,2,1,0:T(4,128)} %param.17) | copy-start | bytes 294916
where the time goes:
time: 40 us; the launch traced here: 39.8 us
  Pallas kernels  34.8 us (87%)
  local copies, waits for them, and re-layouts  2.68 us (7%)
  other arithmetic  1.55 us (4%)
  between operations  0.72 us (2%)
    pallas_call x1, Pallas kernels, per_device(): pl.pallas_call(kernel, out_shape=jax.ShapeDtypeStruct(current_image.shape...  34.8 us
    add x1, other arithmetic, per_device(): current_image + step_value * difference  1.55 us
    reshape x1, local copies, waits for them, and re-layouts, per_device(): w_in = jnp.transpose(weight_in, (2, 3, 4, 1, 0)).reshape(54, CH)  1.34 us
    reshape x1, local copies, waits for them, and re-layouts, per_device(): w_out = jnp.transpose(weight_out, (2, 3, 4, 0, 1)).reshape(54, CH)  1.33 us

commit v1 on v0

--- a/solution.py
+++ b/solution.py
@@ -88,12 +88,12 @@
     image, coil, measured, mask_in, steps_in, order_in, w_in, w_mid, w_out,
     perm_in, high_in, low_in, place1_in, place3_in,
     out,
-    img, imgbuf, hsend, hrecv, dsend, drecv,
+    img, imgbuf, hsend, hrecv, dsend, drecv, ssend, srecv,
     rsend, rrecv, zsend, zrecv, esend, erecv, csend, crecv,
     coilv, rolled, meas, maskv, steps, order, win, wmid, wout,
     perm, high, low, place1, place3,
-    w1, w2, w3, rimg, data, xp, f1, f2, gsum, score, cons,
-    local, send_a, recv_a, send_h, recv_h, send_d, recv_d,
+    w1, w2, w3, rimg, data, xp, f1, f2, parts, score, cons,
+    local, send_a, recv_a, send_h, recv_h, send_d, recv_d, send_s, recv_s,
     send_r, recv_r, send_z, recv_z, send_e, recv_e, send_c, recv_c,
 ):
     b = lax.axis_index("band")
@@ -160,48 +160,23 @@
             dsend[side, zside] = jnp.concatenate(
                 [rows[0][z0], rows[0][z0 + 1], rows[1][z0], rows[1][z0 + 1]], axis=0
             ).astype(BF16)
+    for r in range(2):
+        ssend[0, r] = img[0, r, 0:8, :].astype(BF16)
+        ssend[1, r] = img[1, r, 8:16, :].astype(BF16)
 
     def remote(src, dst, ssem, rsem, who):
         return pltpu.make_async_remote_copy(
             src_ref=src, dst_ref=dst, send_sem=ssem, recv_sem=rsem, device_id=who, device_id_type=MESH
         )
 
-    pl.semaphore_wait(barrier, len(partners))
-    halo_copies = []
-    for side in range(2):
-        ds_ = -1 if side == 0 else 1
-        halo_copies.append(
-            remote(hsend.at[side], hrecv.at[1 - side], send_h.at[side], recv_h.at[1 - side], at(0, ds_))
-        )
-        for zside in range(2):
-            db = -1 if zside == 0 else 1
-            i, j = side * 2 + zside, (1 - side) * 2 + (1 - zside)
-            halo_copies.append(
-                remote(dsend.at[side, zside], drecv.at[1 - side, 1 - zside], send_d.at[i], recv_d.at[j], at(db, ds_))
-            )
-    image_copies = [
-        remote(
-            imgbuf.at[pl.ds(own, 2)], imgbuf.at[pl.ds(own, 2)], send_a.at[k - 1], recv_a.at[k - 1], at(k, 0)
-        )
-        for k in range(1, nb)
-    ]
-    for c in halo_copies + image_copies:
-        c.start()
-
-    arrived("scalars")
-    shifts = [steps[order[g]] * (Y // 8) for g in range(NB)]
-    for g in range(NB):
-        arrived(f"coil{g}")
-        for c in range(NC):
-            for r in range(2):
-                rolled[g, c, r] = pltpu.roll(coilv[g, c, r], shifts[g], 1)
-
     arrived("weights")
     lane = lax.broadcasted_iota(jnp.int32, (1, 6 * CH), 1)
     inside = ((lane >= CH) | (s > 0)) & ((lane < 5 * CH) | (s < ns - 1))
-    w1v = jnp.concatenate([dot_nn(place1[r], win[...]) for r in range(6)], axis=1)
+    flat1 = jnp.concatenate([win[t].astype(F32) for t in range(27)], axis=0).astype(BF16)
+    flat3 = jnp.concatenate([wout[t].astype(F32) for t in range(27)], axis=0).astype(BF16)
+    w1v = jnp.concatenate([dot_nn(place1[r], flat1) for r in range(6)], axis=1)
     w1[...] = jnp.where(inside, w1v, 0.0).astype(BF16)
-    w3[...] = jnp.concatenate([dot_nn(place3[r], wout[...]) for r in range(4)], axis=1).astype(BF16)
+    w3[...] = jnp.concatenate([dot_nn(place3[r], flat3) for r in range(4)], axis=1).astype(BF16)
     none = jnp.zeros((CH, CH), F32)
     for dx in range(3):
         for dz in range(3):
@@ -214,6 +189,41 @@
                     w2[pl.ds(sl * 128 + ro * CH, CH), pl.ds(k * 256, 256)] = block
         w2[pl.ds(128, 128), pl.ds((dx * 4) * 256, 256)] = jnp.zeros((128, 256), BF16)
         w2[pl.ds(0, 128), pl.ds((dx * 4 + 3) * 256, 256)] = jnp.zeros((128, 256), BF16)
+
+    pl.semaphore_wait(barrier, len(partners))
+    halo_copies = []
+    for side in range(2):
+        ds_ = -1 if side == 0 else 1
+        halo_copies.append(
+            remote(hsend.at[side], hrecv.at[1 - side], send_h.at[side], recv_h.at[1 - side], at(0, ds_))
+        )
+        for zside in range(2):
+            db = -1 if zside == 0 else 1
+            i, j = side * 2 + zside, (1 - side) * 2 + (1 - zside)
+            halo_copies.append(
+                remote(dsend.at[side, zside], drecv.at[1 - side, 1 - zside], send_d.at[i], recv_d.at[j], at(db, ds_))
+            )
+    for zside in range(2):
+        db = -1 if zside == 0 else 1
+        halo_copies.append(
+            remote(ssend.at[zside], srecv.at[1 - zside], send_s.at[zside], recv_s.at[1 - zside], at(db, 0))
+        )
+    image_copies = [
+        remote(
+            imgbuf.at[pl.ds(own, 2)], imgbuf.at[pl.ds(own, 2)], send_a.at[k - 1], recv_a.at[k - 1], at(k, 0)
+        )
+        for k in range(1, nb)
+    ]
+    for c in halo_copies + image_copies:
+        c.start()
+
+    arrived("scalars")
+    shifts = [steps[order[g]] * (Y // 8) for g in range(NB)]
+    for g in range(NB):
+        arrived(f"coil{g}")
+        for c in range(NC):
+            for r in range(2):
+                rolled[g, c, r] = pltpu.roll(coilv[g, c, r], shifts[g], 1)
 
     for c in image_copies:
         c.wait_recv()
@@ -236,135 +246,6 @@
         return carry
 
     lax.fori_loop(0, NC, collapse, 0)
-
-    for c in halo_copies:
-        c.wait_recv()
-    arrived("perm")
-    low_ok, high_ok = s > 0, s < ns - 1
-    tiles = []
-    for i in range(12):
-        z = i - 2
-        pieces = []
-        if z < 0:
-            slot = lax.max(2 * b - 1, 0)
-            t = 4 + z
-            ok = b > 0
-            halo = [drecv[side, 0] for side in range(2)]
-            offset, stride = (z + 2) * 2, 4
-        elif z > 7:
-            slot = lax.min(2 * b + 2, NB - 1)
-            t = z - 8
-            ok = b < nb - 1
-            halo = [drecv[side, 1] for side in range(2)]
-            offset, stride = (z - 8) * 2, 4
-        else:
-            slot = own + z // 4
-            t = z % 4
-            ok = None
-            halo = None
-        for r in range(2):
-            mine = imgbuf[slot, r].astype(F32)[4 * t : 4 * t + 4, :]
-            if halo is None:
-                below = hrecv[0, r].astype(F32)[2 * z : 2 * z + 2, :]
-                above = hrecv[1, r].astype(F32)[2 * z : 2 * z + 2, :]
-            else:
-                o = r * stride + offset
-                below = halo[0].astype(F32)[o : o + 2, :]
-                above = halo[1].astype(F32)[o : o + 2, :]
-            below = jnp.where(low_ok, below, 0.0)
-            above = jnp.where(high_ok, above, 0.0)
-            pieces += [mine, below, above]
-        tile = jnp.concatenate(pieces, axis=0)
-        if ok is not None:
-            tile = jnp.where(ok, tile, 0.0)
-        tiles.append(tile.astype(BF16))
-    field = jnp.concatenate(tiles, axis=0)
-    for dx in range(3):
-        moved = dot_nt(field, perm[pl.ds(dx * Y, Y), :]).astype(BF16)
-        for i in range(12):
-            xp[pl.ds(i * 48 + dx * 16, 16), :] = moved[16 * i : 16 * i + 16, :]
-
-    sub = lax.broadcasted_iota(jnp.int32, (16, 6 * CH), 0)
-
-    def first(z, carry):
-        x = xp[pl.ds(pl.multiple_of(z * 48, 48), 144), :]
-        inside_z = ((z > 0) | (b > 0)) & ((z < 9) | (b < nb - 1))
-        x = jnp.where(inside_z, x, jnp.zeros_like(x))
-        h = dot_tn(x, w1[...])
-        f = h + h * jnp.tanh(h)
-        f1[z, pl.ds(16, Y), :] = f.astype(BF16)
-        left = jnp.where(sub == 0, 0.0, pltpu.roll(f[Y - 16 :, :], 1, 0))
-        right = jnp.where(sub == 15, 0.0, pltpu.roll(f[:16, :], 15, 0))
-        f1[z, pl.ds(0, 16), :] = left.astype(BF16)
-        f1[z, pl.ds(Y + 16, 16), :] = right.astype(BF16)
-        return carry
-
-    lax.fori_loop(0, 10, first, 0)
-
-    def middle(zp, carry):
-        for rp in range(2):
-            lhs = jnp.concatenate(
-                [
-                    f1[2 * zp + j, pl.ds(16 * dx, Y), pl.ds(rp * 128, 256)]
-                    for dx in range(3)
-                    for j in range(4)
-                ],
-                axis=1,
-            )
-            h = dot_nt(lhs, w2[...])
-            f = (h + h * jnp.tanh(h)).astype(BF16)
-            f2[2 * zp, :, pl.ds(rp * 128, 128)] = f[:, :128]
-            f2[2 * zp + 1, :, pl.ds(rp * 128, 128)] = f[:, 128:]
-        return carry
-
-    lax.fori_loop(0, 4, middle, 0)
-
-    gsum[...] = jnp.zeros_like(gsum)
-
-    def last(z, carry):
-        part = dot_nt(w3[...], f2[z])
-        for dz in range(3):
-            for dx in range(3):
-                o = (dz * 3 + dx) * 16
-                gsum[2 - dx, z + 2 - dz] += part[o : o + 16, :]
-        return carry
-
-    lax.fori_loop(0, 8, last, 0)
-    total = gsum[...].reshape(3, 160, Y)
-    top = total.astype(BF16)
-    rest = (total - top.astype(F32)).astype(BF16)
-    stacked = jnp.concatenate([jnp.concatenate([top[i], rest[i]], axis=0) for i in range(3)], axis=1)
-    both = dot_nn(stacked, perm[...])
-    score[...] = (both[:160] + both[160:]).reshape(10, 16, Y)
-
-    for side in range(2):
-        o = 8 + 2 * side
-        rsend[side] = jnp.concatenate([score[z + 1, o : o + 2, :] for z in range(8)], axis=0).astype(BF16)
-        zi = 0 if side == 0 else 9
-        zsend[side] = score[zi, 0:8, :].astype(BF16)
-        for rside in range(2):
-            o = 8 + 2 * rside
-            pad = jnp.zeros((6, Y), F32)
-            esend[rside, side] = jnp.concatenate([score[zi, o : o + 2, :], pad], axis=0).astype(BF16)
-    score_copies = []
-    for side in range(2):
-        d = -1 if side == 0 else 1
-        score_copies.append(
-            remote(rsend.at[side], rrecv.at[1 - side], send_r.at[side], recv_r.at[1 - side], at(0, d))
-        )
-        for zside in range(2):
-            db = -1 if zside == 0 else 1
-            i, j = side * 2 + zside, (1 - side) * 2 + (1 - zside)
-            score_copies.append(
-                remote(esend.at[side, zside], erecv.at[1 - side, 1 - zside], send_e.at[i], recv_e.at[j], at(db, d))
-            )
-    for side in range(2):
-        d = -1 if side == 0 else 1
-        score_copies.append(
-            remote(zsend.at[side], zrecv.at[1 - side], send_z.at[side], recv_z.at[1 - side], at(d, 0))
-        )
-    for c in score_copies:
-        c.start()
 
     arrived("tables")
     arrived("meas")
@@ -415,6 +296,134 @@
         )
     for c in cons_copies:
         c.start()
+    for c in halo_copies:
+        c.wait_recv()
+    arrived("perm")
+    low_ok, high_ok = s > 0, s < ns - 1
+    tiles = []
+    for i in range(12):
+        z = i - 2
+        pieces = []
+        if z < 0:
+            t = z + 2
+            ok = b > 0
+            halo = [drecv[side, 0] for side in range(2)]
+            offset, stride = (z + 2) * 2, 4
+        elif z > 7:
+            t = z - 8
+            ok = b < nb - 1
+            halo = [drecv[side, 1] for side in range(2)]
+            offset, stride = (z - 8) * 2, 4
+        else:
+            t = z % 4
+            ok = None
+            halo = None
+        for r in range(2):
+            if halo is None:
+                mine = imgbuf[own + z // 4, r].astype(F32)[4 * t : 4 * t + 4, :]
+                below = hrecv[0, r].astype(F32)[2 * z : 2 * z + 2, :]
+                above = hrecv[1, r].astype(F32)[2 * z : 2 * z + 2, :]
+            else:
+                mine = srecv[0 if z < 0 else 1, r].astype(F32)[4 * t : 4 * t + 4, :]
+                o = r * stride + offset
+                below = halo[0].astype(F32)[o : o + 2, :]
+                above = halo[1].astype(F32)[o : o + 2, :]
+            below = jnp.where(low_ok, below, 0.0)
+            above = jnp.where(high_ok, above, 0.0)
+            pieces += [mine, below, above]
+        tile = jnp.concatenate(pieces, axis=0)
+        if ok is not None:
+            tile = jnp.where(ok, tile, 0.0)
+        tiles.append(tile.astype(BF16))
+    field = jnp.concatenate(tiles, axis=0)
+    for dx in range(3):
+        moved = dot_nt(field, perm[pl.ds(dx * Y, Y), :]).astype(BF16)
+        for i in range(12):
+            xp[pl.ds(i * 48 + dx * 16, 16), :] = moved[16 * i : 16 * i + 16, :]
+
+    sub = lax.broadcasted_iota(jnp.int32, (16, 6 * CH), 0)
+
+    for z in range(10):
+        x = xp[pl.ds(z * 48, 144), :]
+        if z == 0:
+            x = jnp.where(b > 0, x, jnp.zeros_like(x))
+        if z == 9:
+            x = jnp.where(b < nb - 1, x, jnp.zeros_like(x))
+        h = dot_tn(x, w1[...])
+        f = h + h * jnp.tanh(h)
+        f1[z, pl.ds(16, Y), :] = f.astype(BF16)
+        left = jnp.where(sub == 0, 0.0, pltpu.roll(f[Y - 16 :, :], 1, 0))
+        right = jnp.where(sub == 15, 0.0, pltpu.roll(f[:16, :], 15, 0))
+        f1[z, pl.ds(0, 16), :] = left.astype(BF16)
+        f1[z, pl.ds(Y + 16, 16), :] = right.astype(BF16)
+
+    def middle(zp, carry):
+        for rp in range(2):
+            lhs = jnp.concatenate(
+                [
+                    f1[2 * zp + j, pl.ds(16 * dx, Y), pl.ds(rp * 128, 256)]
+                    for dx in range(3)
+                    for j in range(4)
+                ],
+                axis=1,
+            )
+            h = dot_nt(lhs, w2[...])
+            f = (h + h * jnp.tanh(h)).astype(BF16)
+            f2[2 * zp, :, pl.ds(rp * 128, 128)] = f[:, :128]
+            f2[2 * zp + 1, :, pl.ds(rp * 128, 128)] = f[:, 128:]
+        return carry
+
+    lax.fori_loop(0, 4, middle, 0)
+
+    for z in range(8):
+        parts[z] = dot_nt(w3[...], f2[z])
+    both = []
+    for dx in range(3):
+        sums = []
+        for zo in range(10):
+            terms = [
+                parts[zo + dz - 2, pl.ds((dz * 3 + dx) * 16, 16), :]
+                for dz in range(3)
+                if 0 <= zo + dz - 2 < 8
+            ]
+            sums.append(functools.reduce(jnp.add, terms))
+        total = jnp.concatenate(sums, axis=0)
+        top = total.astype(BF16)
+        rest = (total - top.astype(F32)).astype(BF16)
+        both.append(jnp.concatenate([top, rest], axis=0))
+    stacked = jnp.concatenate(both[::-1], axis=1)
+    both = dot_nn(stacked, perm[...])
+    score[...] = (both[:160] + both[160:]).reshape(10, 16, Y)
+
+    for side in range(2):
+        o = 8 + 2 * side
+        rsend[side] = jnp.concatenate([score[z + 1, o : o + 2, :] for z in range(8)], axis=0).astype(BF16)
+        zi = 0 if side == 0 else 9
+        zsend[side] = score[zi, 0:8, :].astype(BF16)
+        for rside in range(2):
+            o = 8 + 2 * rside
+            pad = jnp.zeros((6, Y), F32)
+            esend[rside, side] = jnp.concatenate([score[zi, o : o + 2, :], pad], axis=0).astype(BF16)
+    score_copies = []
+    for side in range(2):
+        d = -1 if side == 0 else 1
+        score_copies.append(
+            remote(rsend.at[side], rrecv.at[1 - side], send_r.at[side], recv_r.at[1 - side], at(0, d))
+        )
+        for zside in range(2):
+            db = -1 if zside == 0 else 1
+            i, j = side * 2 + zside, (1 - side) * 2 + (1 - zside)
+            score_copies.append(
+                remote(esend.at[side, zside], erecv.at[1 - side, 1 - zside], send_e.at[i], recv_e.at[j], at(db, d))
+            )
+    for side in range(2):
+        d = -1 if side == 0 else 1
+        score_copies.append(
+            remote(zsend.at[side], zrecv.at[1 - side], send_z.at[side], recv_z.at[1 - side], at(d, 0))
+        )
+    for c in score_copies:
+        c.start()
+
     for c in halo_copies + image_copies:
         c.wait_send()
 
@@ -463,9 +472,9 @@
     weight_mid,
     weight_out,
 ):
-    w_in = jnp.transpose(weight_in, (2, 3, 4, 1, 0)).reshape(54, CH)
+    w_in = jnp.transpose(weight_in, (2, 3, 4, 1, 0)).reshape(27, 2, CH)
     w_mid = jnp.transpose(weight_mid, (2, 3, 4, 0, 1)).reshape(27, CH, CH)
-    w_out = jnp.transpose(weight_out, (2, 3, 4, 0, 1)).reshape(54, CH)
+    w_out = jnp.transpose(weight_out, (2, 3, 4, 0, 1)).reshape(27, 2, CH)
     consts = [jnp.asarray(c) for c in constants()]
     dma = pltpu.SemaphoreType.DMA
     vmem = pltpu.VMEM
@@ -482,6 +491,8 @@
             vmem((2, 2) + tile, BF16),
             vmem((2, 2, 8, Y), BF16),
             vmem((2, 2, 8, Y), BF16),
+            vmem((2, 2, 8, Y), BF16),
+            vmem((2, 2, 8, Y), BF16),
             vmem((2,) + tile, BF16),
             vmem((2,) + tile, BF16),
             vmem((2, 8, Y), BF16),
@@ -496,9 +507,9 @@
             vmem((NS, Y), jnp.int32),
             pltpu.SMEM((NB,), jnp.int32),
             pltpu.SMEM((NB,), jnp.int32),
-            vmem((54, CH), BF16),
+            vmem((27, 2, CH), BF16),
             vmem((27, CH, CH), BF16),
-            vmem((54, CH), BF16),
+            vmem((27, 2, CH), BF16),
             vmem((3 * Y, Y), BF16),
             vmem((Y, 2 * Y), BF16),
             vmem((Y, 2 * Y), BF16),
@@ -512,7 +523,7 @@
             vmem((12 * 48, Y), BF16),
             vmem((10, Y + 32, 6 * CH), BF16),
             vmem((8, Y, 4 * CH), BF16),
-            vmem((3, 10) + tile, F32),
+            vmem((8, 144, Y), F32),
             vmem((10,) + tile, F32),
             vmem((NB, 2) + tile, F32),
             dma((14, 8)),
@@ -522,6 +533,8 @@
             dma((2,)),
             dma((4,)),
             dma((4,)),
+            dma((2,)),
+            dma((2,)),
             dma((2,)),
             dma((2,)),
             dma((2,)),

time: 40 us -> 35.6 us (0.89)
  local copies, waits for them, and re-layouts: 2.68 us -> 0.01 us
  Pallas kernels: 34.8 us -> 33.2 us
    reshape x2 -> x0, local copies, waits for them, and re-layouts: 2.67 us -> none  [the longest x1 1.34 us: per_device(): w_in = jnp.transpose(weight_in, (2, 3, 4, 1, 0)).reshape(54, CH)]
    pallas_call x1, Pallas kernels: 34.8 us -> 33.2 us  [per_device(): pl.pallas_call(kernel, out_shape=jax.ShapeDtypeStruct(current_image.shape...]
where the time goes in v1:
time: 35.6 us; the launch traced here: 35.5 us
  Pallas kernels  33.2 us (93%)
  other arithmetic  1.55 us (4%)
  between operations  0.74 us (2%)
    pallas_call x1, Pallas kernels, per_device(): pl.pallas_call(kernel, out_shape=jax.ShapeDtypeStruct(current_image.shape...  33.2 us
    add x1, other arithmetic, per_device(): current_image + step_value * difference  1.55 us

profile of v1, /device:TPU:1, one launch (start us, length us, event | category | flops | bytes accessed | tf_op | source)
XLA Modules:
  0.0 35.5 jit_solution(146868349714355968)
XLA Ops:
  0.7 0.0 copy-start
  0.7 0.0 copy-start.1
  0.7 33.2 %langevin.1 = f32[2,4,2,4,384]{4,3,2,1,0:T(4,128)} custom-call(f32[2,4,2,4,384]{4,3,2,1,0:T(4,128)} %image.1, bf16[8,4,8,2,4,384]{5,4,3,2,1,0:T(4,128)(2,1)} %coil.1, f32[4,8,2,4,384]{4,3,2,1,0:T(4,128)} %measured.1, s32[4,384]{1,0:T(4,128)} %mask_in.1, s32[8]{0:T(128)} %steps_in.1, s32[8]{0:T(128)} %order_in.1, bf16[27,2,64]{2,1,0:T(2,128)(2,1)} %bitcast.20, ...), custom_call_target="tpu_custom_call" | custom-call | tf_op jit(solution)/shard_map/langevin/pallas_call | solution.py:482
  33.9 0.0 copy-done
  33.9 0.0 copy-done.1
  33.9 1.6 %multiply_add_fusion = f32[2,4,1,8,384]{4,3,2,1,0:T(8,128)} fusion(f32[2,4,1,8,384]{4,3,2,1,0:T(8,128)S(1)} %bitcast.19, f32[2,4,1,8,384]{4,3,2,1,0:T(8,128)S(1)} %bitcast.17, f32[2,4,1,8,384]{4,3,2,1,0:T(8,128)} %bitcast.18, f32[]{:T(128)S(6)} %sqrt.3, f32[]{:T(128)} %bitcast.14), kind=kLoop, calls=%fused_computation | loop fusion | flops 98304 | bytes 393224 | tf_op jit(solution)/shard_map/add | solution.py:554
Async XLA Ops:
  0.7 33.2 %copy-start = (f32[2,4,2,4,384]{4,3,2,1,0:T(4,128)S(1)}, f32[2,4,2,4,384]{4,3,2,1,0:T(4,128)}, u32[]{:S(2)}) copy-start(f32[2,4,2,4,384]{4,3,2,1,0:T(4,128)} %image.1) | copy-start | bytes 294916
  0.7 33.2 %copy-start.1 = (f32[2,4,2,4,384]{4,3,2,1,0:T(4,128)S(1)}, f32[2,4,2,4,384]{4,3,2,1,0:T(4,128)}, u32[]{:S(2)}) copy-start(f32[2,4,2,4,384]{4,3,2,1,0:T(4,128)} %param.17) | copy-start | bytes 294916

commit v2 on v1

--- a/solution.py
+++ b/solution.py
@@ -85,10 +85,10 @@
 
 
 def kernel(
-    image, coil, measured, mask_in, steps_in, order_in, w_in, w_mid, w_out,
+    image, noise_in, step_in, coil, measured, mask_in, steps_in, order_in, w_in, w_mid, w_out,
     perm_in, high_in, low_in, place1_in, place3_in,
     out,
-    img, imgbuf, hsend, hrecv, dsend, drecv, ssend, srecv,
+    img, noise, step, imgbuf, hsend, hrecv, dsend, drecv, ssend, srecv,
     rsend, rrecv, zsend, zrecv, esend, erecv, csend, crecv,
     coilv, rolled, meas, maskv, steps, order, win, wmid, wout,
     perm, high, low, place1, place3,
@@ -106,10 +106,6 @@
 
     partners = [at(k, 0) for k in range(1, nb)] + [at(0, -1), at(0, 1)]
     partners += [at(db, ds_) for db in (-1, 1) for ds_ in (-1, 1)]
-    barrier = pltpu.get_barrier_semaphore()
-    for who in partners:
-        pl.semaphore_signal(barrier, inc=1, device_id=who, device_id_type=MESH)
-
     groups = {}
 
     def fetch(name, index, pairs):
@@ -123,7 +119,11 @@
             c.wait()
 
     fetch("image", 0, [(image.at[g, t], img.at[g, :, pl.ds(4 * t, 4), :]) for g in range(2) for t in range(4)])
-    fetch("scalars", 1, [(steps_in, steps), (order_in, order)])
+    barrier = pltpu.get_barrier_semaphore()
+    for who in partners:
+        pl.semaphore_signal(barrier, inc=1, device_id=who, device_id_type=MESH)
+
+    fetch("scalars", 1, [(steps_in, steps), (order_in, order), (step_in, step)])
     for g in range(NB):
         fetch(
             f"coil{g}",
@@ -142,6 +142,7 @@
         13,
         [(measured.at[t, :, r], meas.at[r, :, pl.ds(4 * t, 4), :]) for t in range(4) for r in range(2)],
     )
+    fetch("noise", 14, [(noise_in.at[g, t], noise.at[g, :, pl.ds(4 * t, 4), :]) for g in range(2) for t in range(4)])
 
     arrived("image")
     own = pl.multiple_of(2 * b, 2)
@@ -169,6 +170,33 @@
             src_ref=src, dst_ref=dst, send_sem=ssem, recv_sem=rsem, device_id=who, device_id_type=MESH
         )
 
+    pl.semaphore_wait(barrier, len(partners))
+    halo_copies = []
+    for side in range(2):
+        ds_ = -1 if side == 0 else 1
+        halo_copies.append(
+            remote(hsend.at[side], hrecv.at[1 - side], send_h.at[side], recv_h.at[1 - side], at(0, ds_))
+        )
+        for zside in range(2):
+            db = -1 if zside == 0 else 1
+            i, j = side * 2 + zside, (1 - side) * 2 + (1 - zside)
+            halo_copies.append(
+                remote(dsend.at[side, zside], drecv.at[1 - side, 1 - zside], send_d.at[i], recv_d.at[j], at(db, ds_))
+            )
+    for zside in range(2):
+        db = -1 if zside == 0 else 1
+        halo_copies.append(
+            remote(ssend.at[zside], srecv.at[1 - zside], send_s.at[zside], recv_s.at[1 - zside], at(db, 0))
+        )
+    image_copies = [
+        remote(
+            imgbuf.at[pl.ds(own, 2)], imgbuf.at[pl.ds(own, 2)], send_a.at[k - 1], recv_a.at[k - 1], at(k, 0)
+        )
+        for k in range(1, nb)
+    ]
+    for c in halo_copies + image_copies:
+        c.start()
+
     arrived("weights")
     lane = lax.broadcasted_iota(jnp.int32, (1, 6 * CH), 1)
     inside = ((lane >= CH) | (s > 0)) & ((lane < 5 * CH) | (s < ns - 1))
@@ -190,33 +218,6 @@
         w2[pl.ds(128, 128), pl.ds((dx * 4) * 256, 256)] = jnp.zeros((128, 256), BF16)
         w2[pl.ds(0, 128), pl.ds((dx * 4 + 3) * 256, 256)] = jnp.zeros((128, 256), BF16)
 
-    pl.semaphore_wait(barrier, len(partners))
-    halo_copies = []
-    for side in range(2):
-        ds_ = -1 if side == 0 else 1
-        halo_copies.append(
-            remote(hsend.at[side], hrecv.at[1 - side], send_h.at[side], recv_h.at[1 - side], at(0, ds_))
-        )
-        for zside in range(2):
-            db = -1 if zside == 0 else 1
-            i, j = side * 2 + zside, (1 - side) * 2 + (1 - zside)
-            halo_copies.append(
-                remote(dsend.at[side, zside], drecv.at[1 - side, 1 - zside], send_d.at[i], recv_d.at[j], at(db, ds_))
-            )
-    for zside in range(2):
-        db = -1 if zside == 0 else 1
-        halo_copies.append(
-            remote(ssend.at[zside], srecv.at[1 - zside], send_s.at[zside], recv_s.at[1 - zside], at(db, 0))
-        )
-    image_copies = [
-        remote(
-            imgbuf.at[pl.ds(own, 2)], imgbuf.at[pl.ds(own, 2)], send_a.at[k - 1], recv_a.at[k - 1], at(k, 0)
-        )
-        for k in range(1, nb)
-    ]
-    for c in halo_copies + image_copies:
-        c.start()
-
     arrived("scalars")
     shifts = [steps[order[g]] * (Y // 8) for g in range(NB)]
     for g in range(NB):
@@ -265,37 +266,6 @@
     keep = jnp.concatenate([jnp.broadcast_to(keep[t : t + 1], (4, Y)) for t in range(4)], axis=0)[None]
     data[0] = keep * ((re_c + im_s).reshape(NC, 16, Y) - meas[0])
     data[1] = keep * ((im_c - re_s).reshape(NC, 16, Y) - meas[1])
-    re_c, re_s, im_c, im_s = transform(data[...])
-    data[0] = (re_c - im_s).reshape(NC, 16, Y)
-    data[1] = (im_c + re_s).reshape(NC, 16, Y)
-
-    for g in range(NB):
-        real = jnp.zeros((16, Y), F32)
-        imag = jnp.zeros((16, Y), F32)
-        for c in range(NC):
-            a_re = rolled[g, c, 0].astype(F32)
-            a_im = rolled[g, c, 1].astype(F32)
-            real += a_re * data[0, c] + a_im * data[1, c]
-            imag += a_re * data[1, c] - a_im * data[0, c]
-        back = lax.rem(Y - shifts[g], Y)
-        cons[g, 0] = pltpu.roll(real, back, 1)
-        cons[g, 1] = pltpu.roll(imag, back, 1)
-        csend[g, 0] = cons[g, 0].astype(BF16)
-        csend[g, 1] = cons[g, 1].astype(BF16)
-    cons_copies = []
-    for k in range(1, nb):
-        peer = lax.rem(b + k, nb)
-        cons_copies.append(
-            remote(
-                csend.at[pl.ds(pl.multiple_of(2 * peer, 2), 2)],
-                crecv.at[k - 1],
-                send_c.at[k - 1],
-                recv_c.at[k - 1],
-                at(k, 0),
-            )
-        )
-    for c in cons_copies:
-        c.start()
     for c in halo_copies:
         c.wait_recv()
     arrived("perm")
@@ -424,9 +394,45 @@
     for c in score_copies:
         c.start()
 
+    re_c, re_s, im_c, im_s = transform(data[...])
+    data[0] = (re_c - im_s).reshape(NC, 16, Y)
+    data[1] = (im_c + re_s).reshape(NC, 16, Y)
+
+    cons_copies = []
+    for k in (1, 2, 3, 0):
+        peer = lax.rem(b + k, nb)
+        for i in range(2):
+            g = 2 * peer + i
+            real = jnp.zeros((16, Y), F32)
+            imag = jnp.zeros((16, Y), F32)
+            for c in range(NC):
+                a_re = rolled[g, c, 0].astype(F32)
+                a_im = rolled[g, c, 1].astype(F32)
+                real += a_re * data[0, c] + a_im * data[1, c]
+                imag += a_re * data[1, c] - a_im * data[0, c]
+            back = lax.rem(Y - steps[order[g]] * (Y // 8), Y)
+            real = pltpu.roll(real, back, 1)
+            imag = pltpu.roll(imag, back, 1)
+            if k > 0:
+                csend[k - 1, i, 0] = real.astype(BF16)
+                csend[k - 1, i, 1] = imag.astype(BF16)
+            else:
+                cons[i, 0] = real
+                cons[i, 1] = imag
+        if k > 0:
+            copy = remote(csend.at[k - 1], crecv.at[k - 1], send_c.at[k - 1], recv_c.at[k - 1], at(k, 0))
+            copy.start()
+            cons_copies.append(copy)
+
     for c in halo_copies + image_copies:
         c.wait_send()
 
+    arrived("noise")
+    size = jnp.full((16, Y), step[0], F32)
+    spread = jnp.sqrt(2.0 * size)
+    for g in range(2):
+        for r in range(2):
+            cons[g, r] = img[g, r] + spread * noise[g, r] - size * cons[g, r]
     for c in score_copies:
         c.wait_recv()
     for c in cons_copies:
@@ -435,9 +441,9 @@
     for g in range(2):
         consistency = []
         for r in range(2):
-            v = cons[own + g, r]
+            v = cons[g, r]
             for k in range(1, nb):
-                v = v + crecv[k - 1, g, r].astype(F32)
+                v = v - size * crecv[k - 1, g, r].astype(F32)
             consistency.append(v)
         for t in range(4):
             z = g * 4 + t
@@ -454,7 +460,7 @@
                 [below[0:1], gap, above[0:1], below[1:2], gap, above[1:2]], axis=0
             )
             for r in range(2):
-                out[g, t, r] = v[4 * r : 4 * r + 4, :] - consistency[r][4 * t : 4 * t + 4, :]
+                out[g, t, r] = size[0:4] * v[4 * r : 4 * r + 4, :] + consistency[r][4 * t : 4 * t + 4, :]
     for c in score_copies + cons_copies:
         c.wait_send()
 
@@ -479,13 +485,15 @@
     dma = pltpu.SemaphoreType.DMA
     vmem = pltpu.VMEM
     tile = (16, Y)
-    difference = pl.pallas_call(
+    return pl.pallas_call(
         kernel,
         out_shape=jax.ShapeDtypeStruct(current_image.shape, F32),
-        in_specs=[pl.BlockSpec(memory_space=pl.ANY)] * 14,
+        in_specs=[pl.BlockSpec(memory_space=pl.ANY)] * 16,
         out_specs=pl.BlockSpec(memory_space=pltpu.VMEM),
         scratch_shapes=[
             vmem((2, 2) + tile, F32),
+            vmem((2, 2) + tile, F32),
+            pltpu.SMEM((1,), F32),
             vmem((NB, 2) + tile, BF16),
             vmem((2, 2) + tile, BF16),
             vmem((2, 2) + tile, BF16),
@@ -499,7 +507,7 @@
             vmem((2, 8, Y), BF16),
             vmem((2, 2, 8, Y), BF16),
             vmem((2, 2, 8, Y), BF16),
-            vmem((NB, 2) + tile, BF16),
+            vmem((3, 2, 2) + tile, BF16),
             vmem((3, 2, 2) + tile, BF16),
             vmem((NB, NC, 2) + tile, BF16),
             vmem((NB, NC, 2) + tile, BF16),
@@ -525,8 +533,8 @@
             vmem((8, Y, 4 * CH), BF16),
             vmem((8, 144, Y), F32),
             vmem((10,) + tile, F32),
-            vmem((NB, 2) + tile, F32),
-            dma((14, 8)),
+            vmem((2, 2) + tile, F32),
+            dma((15, 8)),
             dma((3,)),
             dma((3,)),
             dma((2,)),
@@ -547,11 +555,9 @@
         compiler_params=pltpu.CompilerParams(collective_id=0, has_side_effects=True),
         name="langevin",
     )(
-        current_image, coil_maps, measured_kspace, sample_mask, caipi_steps, band_order,
+        current_image, langevin_noise, step_size, coil_maps, measured_kspace, sample_mask, caipi_steps, band_order,
         w_in, w_mid, w_out, *consts,
     )
-    step_value = step_size[0]
-    return current_image + step_value * difference + jnp.sqrt(2.0 * step_value) * langevin_noise
 
 
 def solution(mesh):

time: 35.6 us -> 34.7 us (0.975)
  other arithmetic: 1.55 us -> 0 us
  local copies, waits for them, and re-layouts: 0.01 us -> 1.54 us
  Pallas kernels: 33.2 us -> 32.3 us
    add x1 -> x0, other arithmetic: 1.55 us -> none  [per_device(): current_image + step_value * difference]
    unnamed x4 -> x1, local copies, waits for them, and re-layouts: 0.01 us -> 1.54 us
    pallas_call x1, Pallas kernels: 33.2 us -> 32.3 us  [per_device(): pl.pallas_call(kernel, out_shape=jax.ShapeDtypeStruct(current_image.shape...]
where the time goes in v2:
time: 34.7 us; the launch traced here: 34.5 us
  Pallas kernels  32.3 us (93%)
  local copies, waits for them, and re-layouts  1.54 us (4%)
  between operations  0.66 us (2%)
    pallas_call x1, Pallas kernels, per_device(): pl.pallas_call(kernel, out_shape=jax.ShapeDtypeStruct(current_image.shape...  32.3 us
    unnamed x1, local copies, waits for them, and re-layouts  1.54 us

profile of v2, /device:TPU:1, one launch (start us, length us, event | category | flops | bytes accessed | tf_op | source)
XLA Modules:
  0.0 34.5 jit_solution(12586446539230303177)
XLA Ops:
  0.7 32.3 %langevin.1 = f32[2,4,2,4,384]{4,3,2,1,0:T(4,128)} custom-call(f32[2,4,2,4,384]{4,3,2,1,0:T(4,128)} %image.1, f32[2,4,2,4,384]{4,3,2,1,0:T(4,128)} %noise_in.1, f32[1]{0:T(128)S(6)} %copy.18.step_in, bf16[8,4,8,2,4,384]{5,4,3,2,1,0:T(4,128)(2,1)} %coil.1, f32[4,8,2,4,384]{4,3,2,1,0:T(4,128)} %measured.1, s32[4,384]{1,0:T(4,128)} %mask_in.1, s32[8]{0:T(128)} %steps_in.1, ...), custom_call_target="tpu_custom_call" | custom-call | tf_op jit(solution)/shard_map/langevin/pallas_call | solution.py:488
  33.0 1.5 %copy.19 = f32[2,4,2,4,384]{4,3,2,1,0:T(4,128)} copy(f32[2,4,2,4,384]{4,3,2,1,0:T(4,128)} %langevin.1) | data formatting | bytes 196608

commit v3 on v2

--- a/solution.py
+++ b/solution.py
@@ -104,8 +104,10 @@
     def at(db, ds_):
         return {"band": lax.rem(b + db + nb, nb), "slab": lax.rem(s + ds_ + ns, ns)}
 
-    partners = [at(k, 0) for k in range(1, nb)] + [at(0, -1), at(0, 1)]
-    partners += [at(db, ds_) for db in (-1, 1) for ds_ in (-1, 1)]
+    low_ok, high_ok = s > 0, s < ns - 1
+    other = 1 - 2 * lax.rem(b, 2)
+    across = lax.rem(b + 2, nb)
+    peers = [across + other, across, b + other]
     groups = {}
 
     def fetch(name, index, pairs):
@@ -120,30 +122,19 @@
 
     fetch("image", 0, [(image.at[g, t], img.at[g, :, pl.ds(4 * t, 4), :]) for g in range(2) for t in range(4)])
     barrier = pltpu.get_barrier_semaphore()
-    for who in partners:
-        pl.semaphore_signal(barrier, inc=1, device_id=who, device_id_type=MESH)
+
+    def greet(ds_):
+        for db in (0, -1, 1):
+            pl.semaphore_signal(barrier, inc=1, device_id=at(db, ds_), device_id_type=MESH)
+
+    pl.when(low_ok)(lambda: greet(-1))
+    pl.when(high_ok)(lambda: greet(1))
+    for peer in peers:
+        pl.semaphore_signal(barrier, inc=1, device_id={"band": peer, "slab": s}, device_id_type=MESH)
 
     fetch("scalars", 1, [(steps_in, steps), (order_in, order), (step_in, step)])
-    for g in range(NB):
-        fetch(
-            f"coil{g}",
-            2 + g,
-            [
-                (coil.at[g, t, :, r], coilv.at[g, :, r, pl.ds(4 * t, 4), :])
-                for t in range(4)
-                for r in range(2)
-            ],
-        )
     fetch("weights", 10, [(w_in, win), (w_mid, wmid), (w_out, wout), (place1_in, place1), (place3_in, place3)])
     fetch("perm", 11, [(perm_in, perm)])
-    fetch("tables", 12, [(high_in, high), (low_in, low), (mask_in, maskv)])
-    fetch(
-        "meas",
-        13,
-        [(measured.at[t, :, r], meas.at[r, :, pl.ds(4 * t, 4), :]) for t in range(4) for r in range(2)],
-    )
-    fetch("noise", 14, [(noise_in.at[g, t], noise.at[g, :, pl.ds(4 * t, 4), :]) for g in range(2) for t in range(4)])
-
     arrived("image")
     own = pl.multiple_of(2 * b, 2)
     for g in range(2):
@@ -170,32 +161,67 @@
             src_ref=src, dst_ref=dst, send_sem=ssem, recv_sem=rsem, device_id=who, device_id_type=MESH
         )
 
-    pl.semaphore_wait(barrier, len(partners))
-    halo_copies = []
+    sides = (s + ns - 1) // ns + (2 * ns - 2 - s) // ns
+    pl.semaphore_wait(barrier, len(peers) + 3 * sides)
+    halo_copies = [[], [], []]
     for side in range(2):
         ds_ = -1 if side == 0 else 1
-        halo_copies.append(
+        halo_copies[side].append(
             remote(hsend.at[side], hrecv.at[1 - side], send_h.at[side], recv_h.at[1 - side], at(0, ds_))
         )
         for zside in range(2):
             db = -1 if zside == 0 else 1
             i, j = side * 2 + zside, (1 - side) * 2 + (1 - zside)
-            halo_copies.append(
+            halo_copies[side].append(
                 remote(dsend.at[side, zside], drecv.at[1 - side, 1 - zside], send_d.at[i], recv_d.at[j], at(db, ds_))
             )
     for zside in range(2):
         db = -1 if zside == 0 else 1
-        halo_copies.append(
+        halo_copies[2].append(
             remote(ssend.at[zside], srecv.at[1 - zside], send_s.at[zside], recv_s.at[1 - zside], at(db, 0))
         )
     image_copies = [
         remote(
-            imgbuf.at[pl.ds(own, 2)], imgbuf.at[pl.ds(own, 2)], send_a.at[k - 1], recv_a.at[k - 1], at(k, 0)
-        )
-        for k in range(1, nb)
+            imgbuf.at[pl.ds(own, 2)], imgbuf.at[pl.ds(own, 2)], send_a.at[k], recv_a.at[k],
+            {"band": peer, "slab": s},
+        )
+        for k, peer in enumerate(peers)
     ]
-    for c in halo_copies + image_copies:
-        c.start()
+
+    def every(copies, verb):
+        for c in copies:
+            getattr(c, verb)()
+
+    def sent_by_side(copies, verb):
+        pl.when(low_ok)(lambda: every(copies[0], verb))
+        pl.when(high_ok)(lambda: every(copies[1], verb))
+        every(copies[2], verb)
+
+    def wait_arrivals(copies):
+        pl.when(high_ok)(lambda: every(copies[0], "wait_recv"))
+        pl.when(low_ok)(lambda: every(copies[1], "wait_recv"))
+        every(copies[2], "wait_recv")
+
+    sent_by_side(halo_copies, "start")
+    every(image_copies, "start")
+
+    for g in range(NB):
+        fetch(
+            f"coil{g}",
+            2 + g,
+            [
+                (coil.at[g, t, :, r], coilv.at[g, :, r, pl.ds(4 * t, 4), :])
+                for t in range(4)
+                for r in range(2)
+            ],
+        )
+    fetch("tables", 12, [(high_in, high), (low_in, low), (mask_in, maskv)])
+    fetch(
+        "meas",
+        13,
+        [(measured.at[t, :, r], meas.at[r, :, pl.ds(4 * t, 4), :]) for t in range(4) for r in range(2)],
+    )
+    fetch("noise", 14, [(noise_in.at[g, t], noise.at[g, :, pl.ds(4 * t, 4), :]) for g in range(2) for t in range(4)])
 
     arrived("weights")
     lane = lax.broadcasted_iota(jnp.int32, (1, 6 * CH), 1)
@@ -226,50 +252,8 @@
             for r in range(2):
                 rolled[g, c, r] = pltpu.roll(coilv[g, c, r], shifts[g], 1)
 
-    for c in image_copies:
-        c.wait_recv()
-    for g in range(NB):
-        for r in range(2):
-            rimg[g, r] = pltpu.roll(imgbuf[g, r].astype(F32), shifts[g], 1)
-
-    def collapse(c, carry):
-        real = jnp.zeros((16, Y), F32)
-        imag = jnp.zeros((16, Y), F32)
-        for g in range(NB):
-            a_re = rolled[g, c, 0].astype(F32)
-            a_im = rolled[g, c, 1].astype(F32)
-            b_re = rimg[g, 0]
-            b_im = rimg[g, 1]
-            real += a_re * b_re - a_im * b_im
-            imag += a_re * b_im + a_im * b_re
-        data[0, c] = real
-        data[1, c] = imag
-        return carry
-
-    lax.fori_loop(0, NC, collapse, 0)
-
-    arrived("tables")
-    arrived("meas")
-
-    def transform(field):
-        flat = field.reshape(2 * NC * 16, Y)
-        top = flat.astype(BF16)
-        rest = (flat - top.astype(F32)).astype(BF16)
-        lhs = jnp.concatenate([top, rest, top], axis=1)
-        rhs = jnp.concatenate([high[...], high[...], low[...]], axis=0)
-        both = dot_nn(lhs, rhs)
-        half = NC * 16
-        return both[:half, :Y], both[:half, Y:], both[half:, :Y], both[half:, Y:]
-
-    re_c, re_s, im_c, im_s = transform(data[...])
-    keep = maskv[...].astype(F32)
-    keep = jnp.concatenate([jnp.broadcast_to(keep[t : t + 1], (4, Y)) for t in range(4)], axis=0)[None]
-    data[0] = keep * ((re_c + im_s).reshape(NC, 16, Y) - meas[0])
-    data[1] = keep * ((im_c - re_s).reshape(NC, 16, Y) - meas[1])
-    for c in halo_copies:
-        c.wait_recv()
+    wait_arrivals(halo_copies)
     arrived("perm")
-    low_ok, high_ok = s > 0, s < ns - 1
     tiles = []
     for i in range(12):
         z = i - 2
@@ -327,7 +311,27 @@
         f1[z, pl.ds(0, 16), :] = left.astype(BF16)
         f1[z, pl.ds(Y + 16, 16), :] = right.astype(BF16)
 
+    every(image_copies, "wait_recv")
+    for g in range(NB):
+        for r in range(2):
+            rimg[g, r] = pltpu.roll(imgbuf[g, r].astype(F32), shifts[g], 1)
+
+    def collapse(c):
+        real = jnp.zeros((16, Y), F32)
+        imag = jnp.zeros((16, Y), F32)
+        for g in range(NB):
+            a_re = rolled[g, c, 0].astype(F32)
+            a_im = rolled[g, c, 1].astype(F32)
+            b_re = rimg[g, 0]
+            b_im = rimg[g, 1]
+            real += a_re * b_re - a_im * b_im
+            imag += a_re * b_im + a_im * b_re
+        data[0, c] = real
+        data[1, c] = imag
+
     def middle(zp, carry):
+        for i in range(2):
+            collapse(2 * zp + i)
         for rp in range(2):
             lhs = jnp.concatenate(
                 [
@@ -374,33 +378,49 @@
             o = 8 + 2 * rside
             pad = jnp.zeros((6, Y), F32)
             esend[rside, side] = jnp.concatenate([score[zi, o : o + 2, :], pad], axis=0).astype(BF16)
-    score_copies = []
+    score_copies = [[], [], []]
     for side in range(2):
         d = -1 if side == 0 else 1
-        score_copies.append(
+        score_copies[side].append(
             remote(rsend.at[side], rrecv.at[1 - side], send_r.at[side], recv_r.at[1 - side], at(0, d))
         )
         for zside in range(2):
             db = -1 if zside == 0 else 1
             i, j = side * 2 + zside, (1 - side) * 2 + (1 - zside)
-            score_copies.append(
+            score_copies[side].append(
                 remote(esend.at[side, zside], erecv.at[1 - side, 1 - zside], send_e.at[i], recv_e.at[j], at(db, d))
             )
     for side in range(2):
         d = -1 if side == 0 else 1
-        score_copies.append(
+        score_copies[2].append(
             remote(zsend.at[side], zrecv.at[1 - side], send_z.at[side], recv_z.at[1 - side], at(d, 0))
         )
-    for c in score_copies:
-        c.start()
-
+    sent_by_side(score_copies, "start")
+
+    arrived("tables")
+    arrived("meas")
+
+    def transform(field):
+        flat = field.reshape(2 * NC * 16, Y)
+        top = flat.astype(BF16)
+        rest = (flat - top.astype(F32)).astype(BF16)
+        lhs = jnp.concatenate([top, rest, top], axis=1)
+        rhs = jnp.concatenate([high[...], high[...], low[...]], axis=0)
+        both = dot_nn(lhs, rhs)
+        half = NC * 16
+        return both[:half, :Y], both[:half, Y:], both[half:, :Y], both[half:, Y:]
+
+    re_c, re_s, im_c, im_s = transform(data[...])
+    keep = maskv[...].astype(F32)
+    keep = jnp.concatenate([jnp.broadcast_to(keep[t : t + 1], (4, Y)) for t in range(4)], axis=0)[None]
+    data[0] = keep * ((re_c + im_s).reshape(NC, 16, Y) - meas[0])
+    data[1] = keep * ((im_c - re_s).reshape(NC, 16, Y) - meas[1])
     re_c, re_s, im_c, im_s = transform(data[...])
     data[0] = (re_c - im_s).reshape(NC, 16, Y)
     data[1] = (im_c + re_s).reshape(NC, 16, Y)
 
     cons_copies = []
-    for k in (1, 2, 3, 0):
-        peer = lax.rem(b + k, nb)
+    for k, peer in enumerate(peers + [b]):
         for i in range(2):
             g = 2 * peer + i
             real = jnp.zeros((16, Y), F32)
@@ -413,19 +433,20 @@
             back = lax.rem(Y - steps[order[g]] * (Y // 8), Y)
             real = pltpu.roll(real, back, 1)
             imag = pltpu.roll(imag, back, 1)
-            if k > 0:
-                csend[k - 1, i, 0] = real.astype(BF16)
-                csend[k - 1, i, 1] = imag.astype(BF16)
+            if k < 3:
+                csend[k, i, 0] = real.astype(BF16)
+                csend[k, i, 1] = imag.astype(BF16)
             else:
                 cons[i, 0] = real
                 cons[i, 1] = imag
-        if k > 0:
-            copy = remote(csend.at[k - 1], crecv.at[k - 1], send_c.at[k - 1], recv_c.at[k - 1], at(k, 0))
+        if k < 3:
+            who = {"band": peer, "slab": s}
+            copy = remote(csend.at[k], crecv.at[k], send_c.at[k], recv_c.at[k], who)
             copy.start()
             cons_copies.append(copy)
 
-    for c in halo_copies + image_copies:
-        c.wait_send()
+    sent_by_side(halo_copies, "wait_send")
+    every(image_copies, "wait_send")
 
     arrived("noise")
     size = jnp.full((16, Y), step[0], F32)
@@ -433,10 +454,8 @@
     for g in range(2):
         for r in range(2):
             cons[g, r] = img[g, r] + spread * noise[g, r] - size * cons[g, r]
-    for c in score_copies:
-        c.wait_recv()
-    for c in cons_copies:
-        c.wait_recv()
+    wait_arrivals(score_copies)
+    every(cons_copies, "wait_recv")
     gap = jnp.zeros((2, Y), F32)
     for g in range(2):
         consistency = []
@@ -461,8 +480,8 @@
             )
             for r in range(2):
                 out[g, t, r] = size[0:4] * v[4 * r : 4 * r + 4, :] + consistency[r][4 * t : 4 * t + 4, :]
-    for c in score_copies + cons_copies:
-        c.wait_send()
+    sent_by_side(score_copies, "wait_send")
+    every(cons_copies, "wait_send")
 
 
 def per_device(

time: 34.7 us -> 31.1 us (0.90)
  the two profiles are of different devices: /device:TPU:1 before, /device:TPU:7 now
where the time goes in v3:
time: 31.1 us; the launch traced here: 30.9 us
  Pallas kernels  28.7 us (92%)
  local copies, waits for them, and re-layouts  1.54 us (5%)
  between operations  0.66 us (2%)
    pallas_call x1, Pallas kernels, per_device(): pl.pallas_call(kernel, out_shape=jax.ShapeDtypeStruct(current_image.shape...  28.7 us
    unnamed x1, local copies, waits for them, and re-layouts  1.54 us

profile of v3, /device:TPU:7, one launch (start us, length us, event | category | flops | bytes accessed | tf_op | source)
XLA Modules:
  0.0 30.9 jit_solution(9059670605859458462)
XLA Ops:
  0.7 28.7 %langevin.1 = f32[2,4,2,4,384]{4,3,2,1,0:T(4,128)} custom-call(f32[2,4,2,4,384]{4,3,2,1,0:T(4,128)} %image.1, f32[2,4,2,4,384]{4,3,2,1,0:T(4,128)} %noise_in.1, f32[1]{0:T(128)S(6)} %copy.18.step_in, bf16[8,4,8,2,4,384]{5,4,3,2,1,0:T(4,128)(2,1)} %coil.1, f32[4,8,2,4,384]{4,3,2,1,0:T(4,128)} %measured.1, s32[4,384]{1,0:T(4,128)} %mask_in.1, s32[8]{0:T(128)} %steps_in.1, ...), custom_call_target="tpu_custom_call" | custom-call | tf_op jit(solution)/shard_map/langevin/pallas_call | solution.py:507
  29.3 1.5 %copy.19 = f32[2,4,2,4,384]{4,3,2,1,0:T(4,128)} copy(f32[2,4,2,4,384]{4,3,2,1,0:T(4,128)} %langevin.1) | data formatting | bytes 196608

commit v4 on v3

--- a/solution.py
+++ b/solution.py
@@ -92,7 +92,7 @@
     rsend, rrecv, zsend, zrecv, esend, erecv, csend, crecv,
     coilv, rolled, meas, maskv, steps, order, win, wmid, wout,
     perm, high, low, place1, place3,
-    w1, w2, w3, rimg, data, xp, f1, f2, parts, score, cons,
+    w1, w2, w2e, w3, rimg, data, xp, f1, f2, parts, score, cons,
     local, send_a, recv_a, send_h, recv_h, send_d, recv_d, send_s, recv_s,
     send_r, recv_r, send_z, recv_z, send_e, recv_e, send_c, recv_c,
 ):
@@ -239,10 +239,15 @@
                 block = taps + [none] if ro == 0 else [none] + taps
                 block = jnp.concatenate(block, axis=1).astype(BF16)
                 for sl in range(2):
-                    k = dx * 4 + dz + sl
-                    w2[pl.ds(sl * 128 + ro * CH, CH), pl.ds(k * 256, 256)] = block
-        w2[pl.ds(128, 128), pl.ds((dx * 4) * 256, 256)] = jnp.zeros((128, 256), BF16)
-        w2[pl.ds(0, 128), pl.ds((dx * 4 + 3) * 256, 256)] = jnp.zeros((128, 256), BF16)
+                    j = dz + sl
+                    if j in (1, 2):
+                        w2[pl.ds(sl * 128 + ro * CH, CH), pl.ds((dx * 2 + j - 1) * 256, 256)] = block
+                    elif dx == 1:
+                        w2[pl.ds(sl * 128 + ro * CH, CH), pl.ds((6 + sl) * 256, 256)] = block
+                    else:
+                        w2e[sl, pl.ds(dx // 2 * 128 + ro * CH, CH), :] = block
+    w2[pl.ds(128, 128), pl.ds(6 * 256, 256)] = jnp.zeros((128, 256), BF16)
+    w2[pl.ds(0, 128), pl.ds(7 * 256, 256)] = jnp.zeros((128, 256), BF16)
 
     arrived("scalars")
     shifts = [steps[order[g]] * (Y // 8) for g in range(NB)]
@@ -333,18 +338,14 @@
         for i in range(2):
             collapse(2 * zp + i)
         for rp in range(2):
-            lhs = jnp.concatenate(
-                [
-                    f1[2 * zp + j, pl.ds(16 * dx, Y), pl.ds(rp * 128, 256)]
-                    for dx in range(3)
-                    for j in range(4)
-                ],
-                axis=1,
-            )
-            h = dot_nt(lhs, w2[...])
-            f = (h + h * jnp.tanh(h)).astype(BF16)
-            f2[2 * zp, :, pl.ds(rp * 128, 128)] = f[:, :128]
-            f2[2 * zp + 1, :, pl.ds(rp * 128, 128)] = f[:, 128:]
+            lanes = pl.ds(rp * 128, 256)
+            views = [f1[2 * zp + j, pl.ds(16 * dx, Y), lanes] for dx in range(3) for j in (1, 2)]
+            views += [f1[2 * zp + j, pl.ds(16, Y), lanes] for j in (0, 3)]
+            h = dot_nt(jnp.concatenate(views, axis=1), w2[...])
+            for sl in range(2):
+                side = dot_nt(f1[2 * zp + 3 * sl, :, lanes], w2e[sl])
+                v = h[:, sl * 128 : sl * 128 + 128] + side[:Y, :128] + side[32:, 128:]
+                f2[2 * zp + sl, :, pl.ds(rp * 128, 128)] = (v + v * jnp.tanh(v)).astype(BF16)
         return carry
 
     lax.fori_loop(0, 4, middle, 0)
@@ -543,7 +544,8 @@
             vmem((6, 144, 54), BF16),
             vmem((4, 144, 54), BF16),
             vmem((144, 6 * CH), BF16),
-            vmem((256, 12 * 256), BF16),
+            vmem((256, 8 * 256), BF16),
+            vmem((2, 256, 256), BF16),
             vmem((144, 4 * CH), BF16),
             vmem((NB, 2) + tile, F32),
             vmem((2, NC) + tile, F32),
@@ -571,11 +573,16 @@
             dma((3,)),
             dma((3,)),
         ],
-        compiler_params=pltpu.CompilerParams(collective_id=0, has_side_effects=True),
+        compiler_params=pltpu.CompilerParams(collective_id=0, has_side_effects=True, vmem_limit_bytes=40 * 1024 * 1024),
         name="langevin",
     )(
-        current_image, langevin_noise, step_size, coil_maps, measured_kspace, sample_mask, caipi_steps, band_order,
-        w_in, w_mid, w_out, *consts,
+        *[
+            v if v.shape == (1,) else pltpu.with_memory_space_constraint(v, pltpu.HBM)
+            for v in (
+                current_image, langevin_noise, step_size, coil_maps, measured_kspace, sample_mask,
+                caipi_steps, band_order, w_in, w_mid, w_out, *consts,
+            )
+        ]
     )
 
 

time: 31.1 us -> 28.7 us (0.923)
  Pallas kernels: 28.7 us -> 27.3 us
  local copies, waits for them, and re-layouts: 1.54 us -> 0.64 us
    pallas_call x1, Pallas kernels: 28.7 us -> 27.3 us  [per_device(): pl.pallas_call(kernel, out_shape=jax.ShapeDtypeStruct(current_image.shape...]
    unnamed x1, local copies, waits for them, and re-layouts: 1.54 us -> 0.64 us
where the time goes in v4:
time: 28.7 us; the launch traced here: 28.6 us
  Pallas kernels  27.3 us (95%)
  between operations  0.66 us (2%)
  local copies, waits for them, and re-layouts  0.64 us (2%)
    pallas_call x1, Pallas kernels, per_device(): pl.pallas_call(kernel, out_shape=jax.ShapeDtypeStruct(current_image.shape...  27.3 us
    unnamed x1, local copies, waits for them, and re-layouts  0.64 us

profile of v4, /device:TPU:7, one launch (start us, length us, event | category | flops | bytes accessed | tf_op | source)
XLA Modules:
  0.0 28.6 jit_solution(5199471435436247553)
XLA Ops:
  0.7 27.3 %langevin.1 = f32[2,4,2,4,384]{4,3,2,1,0:T(4,128)S(1)} custom-call(f32[2,4,2,4,384]{4,3,2,1,0:T(4,128)} %image.1, f32[2,4,2,4,384]{4,3,2,1,0:T(4,128)} %noise_in.1, f32[1]{0:T(128)S(6)} %copy.18.step_in, bf16[8,4,8,2,4,384]{5,4,3,2,1,0:T(4,128)(2,1)} %coil.1, f32[4,8,2,4,384]{4,3,2,1,0:T(4,128)} %measured.1, s32[4,384]{1,0:T(4,128)} %mask_in.1, s32[8]{0:T(128)} %steps_in.1, ...), custom_call_target="tpu_custom_call" | custom-call | tf_op jit(solution)/shard_map/langevin/pallas_call | solution.py:508
  27.9 0.6 %copy.19 = f32[2,4,2,4,384]{4,3,2,1,0:T(4,128)} copy(f32[2,4,2,4,384]{4,3,2,1,0:T(4,128)S(1)} %langevin.1) | data formatting | bytes 196608

commit v5 on v4

--- a/solution.py
+++ b/solution.py
@@ -47,7 +47,7 @@
                         if 0 <= dy <= 2:
                             t = ((dz * 3 + dy) * 3 + dx) * 2 + ch
                             place_in[ro, dz * 48 + dx * 16 + ch * 8 + i, t] = 0.5
-    place_out = np.zeros((4, 144, 54), np.float32)
+    place_out = np.zeros((4, 160, 54), np.float32)
     for rin in range(4):
         for dz in range(3):
             for dx in range(3):
@@ -57,12 +57,12 @@
                         if 0 <= dy <= 2:
                             t = ((dz * 3 + dy) * 3 + dx) * 2 + ch
                             if ro == -1:
-                                m = 8 + ch
+                                m = ch
                             elif ro == 4:
-                                m = 10 + ch
+                                m = 2 + ch
                             else:
-                                m = ch * 4 + ro
-                            place_out[rin, (dz * 3 + dx) * 16 + m, t] = 1.0
+                                m = 80 + ch * 4 + ro
+                            place_out[rin, (dz * 3 + dx) * 8 + m, t] = 1.0
     return (
         perm.reshape(3 * Y, Y).astype(BF16),
         high,
@@ -335,8 +335,6 @@
         data[1, c] = imag
 
     def middle(zp, carry):
-        for i in range(2):
-            collapse(2 * zp + i)
         for rp in range(2):
             lanes = pl.ds(rp * 128, 256)
             views = [f1[2 * zp + j, pl.ds(16 * dx, Y), lanes] for dx in range(3) for j in (1, 2)]
@@ -350,35 +348,35 @@
 
     lax.fori_loop(0, 4, middle, 0)
 
-    for z in range(8):
-        parts[z] = dot_nt(w3[...], f2[z])
-    both = []
-    for dx in range(3):
-        sums = []
-        for zo in range(10):
-            terms = [
-                parts[zo + dz - 2, pl.ds((dz * 3 + dx) * 16, 16), :]
-                for dz in range(3)
-                if 0 <= zo + dz - 2 < 8
-            ]
-            sums.append(functools.reduce(jnp.add, terms))
-        total = jnp.concatenate(sums, axis=0)
-        top = total.astype(BF16)
-        rest = (total - top.astype(F32)).astype(BF16)
-        both.append(jnp.concatenate([top, rest], axis=0))
-    stacked = jnp.concatenate(both[::-1], axis=1)
-    both = dot_nn(stacked, perm[...])
-    score[...] = (both[:160] + both[160:]).reshape(10, 16, Y)
-
+    def scores(half):
+        for z in range(8):
+            parts[half, z] = dot_nt(w3[pl.ds(80 * half, 80), :], f2[z])
+        both = []
+        for dx in range(3):
+            sums = []
+            for zo in range(10):
+                terms = [
+                    parts[half, zo + dz - 2, pl.ds((dz * 3 + dx) * 8, 8), :]
+                    for dz in range(3)
+                    if 0 <= zo + dz - 2 < 8
+                ]
+                sums.append(functools.reduce(jnp.add, terms))
+            total = jnp.concatenate(sums, axis=0)
+            top = total.astype(BF16)
+            rest = (total - top.astype(F32)).astype(BF16)
+            both.append(jnp.concatenate([top, rest], axis=0))
+        both = dot_nn(jnp.concatenate(both[::-1], axis=1), perm[...])
+        score[half] = (both[:80] + both[80:]).reshape(10, 8, Y)
+
+    scores(0)
     for side in range(2):
-        o = 8 + 2 * side
-        rsend[side] = jnp.concatenate([score[z + 1, o : o + 2, :] for z in range(8)], axis=0).astype(BF16)
+        o = 2 * side
+        rsend[side] = jnp.concatenate([score[0, z + 1, o : o + 2, :] for z in range(8)], axis=0).astype(BF16)
         zi = 0 if side == 0 else 9
-        zsend[side] = score[zi, 0:8, :].astype(BF16)
         for rside in range(2):
-            o = 8 + 2 * rside
+            o = 2 * rside
             pad = jnp.zeros((6, Y), F32)
-            esend[rside, side] = jnp.concatenate([score[zi, o : o + 2, :], pad], axis=0).astype(BF16)
+            esend[rside, side] = jnp.concatenate([score[0, zi, o : o + 2, :], pad], axis=0).astype(BF16)
     score_copies = [[], [], []]
     for side in range(2):
         d = -1 if side == 0 else 1
@@ -396,8 +394,14 @@
         score_copies[2].append(
             remote(zsend.at[side], zrecv.at[1 - side], send_z.at[side], recv_z.at[1 - side], at(d, 0))
         )
-    sent_by_side(score_copies, "start")
-
+    pl.when(low_ok)(lambda: every(score_copies[0], "start"))
+    pl.when(high_ok)(lambda: every(score_copies[1], "start"))
+
+    def collapses(c, carry):
+        collapse(c)
+        return carry
+
+    lax.fori_loop(0, NC, collapses, 0)
     arrived("tables")
     arrived("meas")
 
@@ -446,6 +450,10 @@
             copy.start()
             cons_copies.append(copy)
 
+    scores(1)
+    for side in range(2):
+        zsend[side] = score[1, 9 * side].astype(BF16)
+    every(score_copies[2], "start")
     sent_by_side(halo_copies, "wait_send")
     every(image_copies, "wait_send")
 
@@ -467,7 +475,7 @@
             consistency.append(v)
         for t in range(4):
             z = g * 4 + t
-            v = score[z + 1, 0:8, :]
+            v = score[1, z + 1]
             below = jnp.where(low_ok, rrecv[0].astype(F32)[2 * z : 2 * z + 2, :], 0.0)
             above = jnp.where(high_ok, rrecv[1].astype(F32)[2 * z : 2 * z + 2, :], 0.0)
             if z in (0, 7):
@@ -542,18 +550,18 @@
             vmem((Y, 2 * Y), BF16),
             vmem((Y, 2 * Y), BF16),
             vmem((6, 144, 54), BF16),
-            vmem((4, 144, 54), BF16),
+            vmem((4, 160, 54), BF16),
             vmem((144, 6 * CH), BF16),
             vmem((256, 8 * 256), BF16),
             vmem((2, 256, 256), BF16),
-            vmem((144, 4 * CH), BF16),
+            vmem((160, 4 * CH), BF16),
             vmem((NB, 2) + tile, F32),
             vmem((2, NC) + tile, F32),
             vmem((12 * 48, Y), BF16),
             vmem((10, Y + 32, 6 * CH), BF16),
             vmem((8, Y, 4 * CH), BF16),
-            vmem((8, 144, Y), F32),
-            vmem((10,) + tile, F32),
+            vmem((2, 8, 80, Y), F32),
+            vmem((2, 10, 8, Y), F32),
             vmem((2, 2) + tile, F32),
             dma((15, 8)),
             dma((3,)),

time: 28.7 us -> 28.1 us (0.979)
  Pallas kernels: 27.3 us -> 26.6 us
    pallas_call x1, Pallas kernels: 27.3 us -> 26.6 us  [per_device(): pl.pallas_call(kernel, out_shape=jax.ShapeDtypeStruct(current_image.shape...]
where the time goes in v5:
time: 28.1 us; the launch traced here: 28 us
  Pallas kernels  26.6 us (95%)
  between operations  0.66 us (2%)
  local copies, waits for them, and re-layouts  0.64 us (2%)
    pallas_call x1, Pallas kernels, per_device(): pl.pallas_call(kernel, out_shape=jax.ShapeDtypeStruct(current_image.shape...  26.6 us
    unnamed x1, local copies, waits for them, and re-layouts  0.64 us

profile of v5, /device:TPU:7, one launch (start us, length us, event | category | flops | bytes accessed | tf_op | source)
XLA Modules:
  0.0 28.0 jit_solution(11981234658670580366)
XLA Ops:
  0.7 26.6 %langevin.1 = f32[2,4,2,4,384]{4,3,2,1,0:T(4,128)S(1)} custom-call(f32[2,4,2,4,384]{4,3,2,1,0:T(4,128)} %image.1, f32[2,4,2,4,384]{4,3,2,1,0:T(4,128)} %noise_in.1, f32[1]{0:T(128)S(6)} %copy.18.step_in, bf16[8,4,8,2,4,384]{5,4,3,2,1,0:T(4,128)(2,1)} %coil.1, f32[4,8,2,4,384]{4,3,2,1,0:T(4,128)} %measured.1, s32[4,384]{1,0:T(4,128)} %mask_in.1, s32[8]{0:T(128)} %steps_in.1, ...), custom_call_target="tpu_custom_call" | custom-call | tf_op jit(solution)/shard_map/langevin/pallas_call | solution.py:516
  27.3 0.6 %copy.19 = f32[2,4,2,4,384]{4,3,2,1,0:T(4,128)} copy(f32[2,4,2,4,384]{4,3,2,1,0:T(4,128)S(1)} %langevin.1) | data formatting | bytes 196608
